TPU v7x, 512 devices: a whole 4x8x8 slice. The times are simulated.
512 devices in a mesh: dom: 32 (over y, x), orient: 16 (over z, core).
Axes of the slice: x: 4, y: 8, z: 8, core: 2. Of those that a mesh axis runs over, the one named last changes fastest.
Arguments:
- particles: bfloat16 [256, 2, 8192], P('dom'), may hold values from -4 to 4
- references: bfloat16 [256, 2, 8192], P('orient'), may hold values from -1.7 to 1.7
- phases: float32 [16, 8192], replicated, may hold values from -3.1416 to 3.1416
- mask: int32 [256, 256], P('dom', 'orient'), may hold values from 0 to 1, as said below
- ctf_group: int32 [256], replicated, may hold values from 0 to 63
- ctf_table: float32 [64, 64], replicated, may hold values from 0.1 to 1
- shell_index: int32 [8192], replicated, may hold values from 0 to 63
- sigma2: float32 [64], replicated, may hold values from 8 to 32
Outputs:
- posterior: float32 [256, 16, 256], P('dom', None, 'orient')
- image_sums: float32 [256, 2, 8192], P('orient', None, 'dom')
- ctf_weights: float32 [256, 64], P('orient')
- shell_noise: float32 [64], replicated
Inputs may be any that keep to these rules, and one draw needn't show every extreme that they name: `mask`: every particle allows at least one orientation.
All inputs are finite; a program needn't handle non-finite values.
Results may differ from a plain program's by a relative error of at most 0.0041.
Values may be sent and summed in bfloat16 or wider, within the bound.
A program may use at most 192 MiB of HBM per device.

v0:
```python
import jax
import jax.numpy as jnp
from jax import lax
from jax.sharding import PartitionSpec as P

trans_block = 2


def make_images(planes, ctf_pix, cosine, sine_part):
    real_part = planes[:, 0][:, None, :]
    imag_part = planes[:, 1][:, None, :]
    shifted_real = real_part * cosine[None] - imag_part * sine_part[None]
    shifted_imag = real_part * sine_part[None] + imag_part * cosine[None]
    factor = ctf_pix[:, None, :]
    return jnp.stack([factor * shifted_real, factor * shifted_imag], axis=2).astype(jnp.bfloat16)


def on_device(particles, references, phases, mask, ctf_group, ctf_table, shell_index, sigma2):
    highest = lax.Precision.HIGHEST
    part_dev = particles.shape[0]
    ori_dev = references.shape[0]
    pixels = shell_index.shape[0]
    shells = ctf_table.shape[1]
    trans_count = phases.shape[0]
    blocks = trans_count // trans_block
    dom_size = lax.axis_size("dom")
    width = pixels // dom_size
    dom_index = lax.axis_index("dom")
    shell_pick = (shell_index[:, None] == jnp.arange(shells, dtype=jnp.int32)[None, :]).astype(
        jnp.float32
    )
    group_pick = (
        ctf_group[:, None] == jnp.arange(ctf_table.shape[0], dtype=jnp.int32)[None, :]
    ).astype(jnp.float32)
    ctf_all = jnp.dot(group_pick, ctf_table, precision=highest)
    ctf_rows = lax.dynamic_slice_in_dim(ctf_all, dom_index * part_dev, part_dev, 0)
    ctf_pix = jnp.dot(ctf_rows, shell_pick.T, precision=highest)
    sigma_pix = jnp.dot(shell_pick, sigma2, precision=highest)
    refs_wide = references.astype(jnp.float32)
    weighted = (refs_wide / sigma_pix).astype(jnp.bfloat16)
    ref_norm = jnp.dot(jnp.sum(refs_wide * refs_wide, axis=1), shell_pick, precision=highest)
    energy = ref_norm / sigma2
    ctf_square = ctf_rows * ctf_rows
    quadratic = 0.5 * jnp.dot(ctf_square, energy.T, precision=highest)
    planes = particles.astype(jnp.float32)
    cosines = jnp.cos(phases)
    sine_rows = jnp.sin(phases)

    def score_block(index):
        first = index * trans_block
        images = make_images(
            planes,
            ctf_pix,
            lax.dynamic_slice_in_dim(cosines, first, trans_block, 0),
            lax.dynamic_slice_in_dim(sine_rows, first, trans_block, 0),
        )
        cross = jnp.einsum("ptcx,ocx->pto", images, weighted, preferred_element_type=jnp.float32)
        return cross - quadratic[:, None, :]

    stacked = lax.map(score_block, jnp.arange(blocks, dtype=jnp.int32))
    scores = jnp.moveaxis(stacked, 0, 1).reshape(part_dev, trans_count, ori_dev)
    scores = jnp.where((mask == 1)[:, None, :], scores, -1e30)
    local_peak = jnp.max(scores, axis=(1, 2))
    peak = lax.pmax(local_peak, "orient")
    total = lax.psum(jnp.sum(jnp.exp(scores - peak[:, None, None]), axis=(1, 2)), "orient")
    posterior = jnp.exp(scores - peak[:, None, None]) / total[:, None, None]
    post_half = posterior.astype(jnp.bfloat16)
    weight_rows = jnp.sum(posterior, axis=1)
    ctf_part = jnp.dot(weight_rows.T, ctf_square, precision=highest)
    part_norm = jnp.dot(jnp.sum(planes * planes, axis=1), shell_pick, precision=highest)
    term_one = jnp.sum(part_norm * jnp.sum(weight_rows, axis=1)[:, None], axis=0)
    term_three = jnp.sum(ctf_part * ref_norm, axis=0)
    start_pix = dom_index * width
    pick_cols = lax.dynamic_slice_in_dim(shell_pick, start_pix, width, 0)

    def add_block(index, running):
        first = index * trans_block
        images = make_images(
            planes,
            ctf_pix,
            lax.dynamic_slice_in_dim(cosines, first, trans_block, 0),
            lax.dynamic_slice_in_dim(sine_rows, first, trans_block, 0),
        )
        weights = lax.dynamic_slice_in_dim(post_half, first, trans_block, 1)
        return running + jnp.einsum(
            "pto,ptcx->ocx", weights, images, preferred_element_type=jnp.float32
        )

    partial_sums = lax.fori_loop(0, blocks, add_block, jnp.zeros((ori_dev, 2, pixels), jnp.float32))
    image_sums = lax.psum_scatter(partial_sums, "dom", scatter_dimension=2, tiled=True)
    ref_cols = lax.dynamic_slice_in_dim(refs_wide, start_pix, width, 2)
    term_two = -2.0 * jnp.dot(
        jnp.sum(image_sums * ref_cols, axis=(0, 1)), pick_cols, precision=highest
    )
    ctf_weights = lax.psum(ctf_part, "dom")
    shell_total = lax.psum(term_one + term_two + term_three, ("dom", "orient"))
    divisor = part_dev * dom_size * pixels / shells
    return (posterior, image_sums, ctf_weights, shell_total / divisor)


def solution(mesh):
    return jax.shard_map(
        on_device,
        mesh=mesh,
        in_specs=(
            P("dom", None, None),
            P("orient", None, None),
            P(),
            P("dom", "orient"),
            P(),
            P(),
            P(),
            P(),
        ),
        out_specs=(P("dom", None, "orient"), P("orient", None, "dom"), P("orient", None), P()),
        check_vma=False,
    )
```

profile of v0, /device:TPU:1, one launch (start us, length us, event | category | flops | bytes accessed | tf_op | source)
XLA Modules:
  0.0 511.5 jit_solution(465495128250471743)
XLA Ops:
  7.3 0.7 broadcast_compare_fusion
  8.0 1.1 copy_convert_fusion
  9.1 2.8 fusion.46
  12.0 0.7 fusion.15
  12.7 1.9 multiply_reduce_fusion
  14.6 1.1 copy.23
  15.7 1.1 fusion.14
  17.1 0.7 fusion.16
  18.0 21.1 %while.24 = (s32[]{:T(128)}, f32[8,8,2,16]{3,1,2,0:T(8,128)S(1)}, f32[8,8192]{1,0:T(8,128)S(1)}, f32[8,2,8192]{2,0,1:T(8,128)S(1)}, s32[8]{0:T(128)S(1)}, /*inde...) while((s32[]{:T(128)}, f32[8,8,2,16]{3,1,2,0:T(8,128)S(1)}, ...), condition=%wide.region_2.3_spmd, body=%wide.region_1.2_spmd.sunk | while | flops 9961734 | bytes 5910755 | solution.py:60
  19.5 0.8 copy-done.4
  22.2 0.8 copy-done.4
  24.8 0.8 copy-done.4
  27.4 0.8 copy-done.4
  30.1 0.8 copy-done.4
  32.7 0.8 copy-done.4
  35.3 0.8 copy-done.4
  38.0 0.8 copy-done.4
  39.2 30.6 %pmax.7 = f32[8]{0:T(128)S(1)} all-reduce(f32[8]{0:T(128)S(1)} %select_reduce_fusion), channel_id=1, replica_groups=mesh['dom'=32,'orient'=16] {'orient'}, use_global_device_ids=true, to_apply=%region_4.5 | all-reduce | flops 8 | bytes 64 | tf_op jit(solution)/shard_map/pmax | solution.py:64
  70.0 25.8 %psum.21 = f32[8]{0:T(128)S(1)} all-reduce(f32[8]{0:T(128)S(1)} %fusion.30), channel_id=1, replica_groups=mesh['dom'=32,'orient'=16] {'orient'}, use_global_device_ids=true, to_apply=%region_6.7 | all-reduce | flops 8 | bytes 64 | tf_op jit(solution)/shard_map/psum | solution.py:65
  95.9 0.7 fusion.45
  96.6 6.0 %while.25 = (s32[]{:T(128)}, f32[16,2,8192]{2,0,1:T(8,128)S(1)}, bf16[8,16,16]{2,1,0:T(8,128)(2,1)S(1)}, f32[8,8192]{1,0:T(8,128)S(1)}, f32[8,2,8192]{2,0,1:T(8,...) while((s32[]{:T(128)}, f32[16,2,8192]{2,0,1:T(8,128)S(1)}, ...), condition=%wide.region_8.9_spmd.clone, body=%wide.region_7.8_spmd.clone.sunk | while | flops 11272199 | bytes 5375669 | solution.py:89
  102.6 31.4 %copy.29 = f32[16,2,8192]{1,0,2:T(8,128)} copy(f32[16,2,8192]{2,0,1:T(8,128)S(1)} %get-tuple-element.176) | data formatting | bytes 2097152
  134.0 46.1 %reshape.85 = f32[8192,32]{1,0:T(8,128)} reshape(f32[8192,16,2]{2,1,0:T(8,128)} %bitcast.18) | data formatting | bytes 2097152
  181.0 0.9 multiply_reduce_fusion.3
  182.3 63.1 %psum.22 = f32[16,64]{1,0:T(8,128)} all-reduce(f32[16,64]{1,0:T(8,128)S(1)} %get-tuple-element.302), channel_id=1, replica_groups=mesh['dom'=32,'orient'=16] {'dom'}, use_global_device_ids=true, to_apply=%region_11.12 | all-reduce | flops 1024 | bytes 8192 | tf_op jit(solution)/shard_map/psum | solution.py:95
  245.5 1.1 fusion.18
  246.6 1.1 iota_compare_fusion
  247.7 150.6 %reduce-scatter.4.cloned.1.call-done = f32[256,32]{1,0:T(8,128)} async-done(((f32[8192,32]{1,0:T(8,128)}), f32[256,32]{1,0:T(8,128)}) %reduce-scatter.4.cloned.1.call-update) | async-done | bytes 32784
  398.3 2.1 reshape.86
  400.5 1.0 copy.30
  401.6 0.8 fusion.21
  402.4 101.8 %psum.23 = f32[64]{0:T(128)S(1)} all-reduce(f32[64]{0:T(128)S(1)} %fusion.21), channel_id=1, replica_groups=mesh['dom'=32,'orient'=16] {'dom','orient'}, use_global_device_ids=true, to_apply=%region_17.18 | all-reduce | flops 64 | bytes 512 | tf_op jit(solution)/shard_map/psum | solution.py:96
  (127 shorter events, 17.8 us)
Async XLA Ops:
  7.2 9.6 %copy-start = (f32[64,64]{1,0:T(8,128)S(1)}, f32[64,64]{1,0:T(8,128)}, u32[]{:S(2)}) copy-start(f32[64,64]{1,0:T(8,128)} %param.17) | copy-start | bytes 49156
  7.2 4.7 copy-start.7
  7.2 4.7 copy-start.12
  7.2 5.5 %copy-start.1 = (bf16[16,2,8192]{2,1,0:T(2,128)(2,1)S(1)}, bf16[16,2,8192]{2,1,0:T(2,128)(2,1)}, u32[]{:S(2)}) copy-start(bf16[16,2,8192]{2,1,0:T(2,128)(2,1)} %param.13) | copy-start | bytes 1572868
  7.2 391.1 %reduce-scatter.4.cloned.1.call-start = ((), (), s32[]{:S(2)}) async-start(), calls=%async_computation.1 | async-start | bytes 4325376
  11.9 4.9 copy-start.11
  17.1 0.9 copy-start.5
  19.2 1.0 copy-start.4
  21.9 1.0 copy-start.4
  24.5 1.0 copy-start.4
  27.2 1.0 copy-start.4
  29.8 1.0 copy-start.4
  32.4 1.0 copy-start.4
  35.0 1.0 copy-start.4
  37.7 1.0 copy-start.4
  95.8 0.8 copy-start.9
  180.1 0.7 copy-start.10
  180.1 1.8 copy-start.2
  180.1 65.3 %copy-start.3 = (bf16[8,2,8192]{2,1,0:T(2,128)(2,1)S(1)}, bf16[8,2,8192]{2,1,0:T(2,128)(2,1)}, u32[]{:S(2)}) copy-start(bf16[8,2,8192]{2,1,0:T(2,128)(2,1)} %param.12) | copy-start | bytes 786436
  180.8 64.8 %copy-start.8 = (s32[8192]{0:T(1024)S(1)}, s32[8192]{0:T(1024)}, u32[]{:S(2)}) copy-start(s32[8192]{0:T(1024)} %param.18) | copy-start | bytes 98308
  401.5 103.2 %copy-start.6 = (f32[16,2,256]{2,1,0:T(2,128)}, f32[16,2,256]{2,1,0:T(2,128)S(1)}, u32[]{:S(2)}) copy-start(f32[16,2,256]{2,1,0:T(2,128)S(1)} %copy.30) | copy-start | bytes 98308
Sparse Core Ops, SparseCore 0:
  180.3 218.0 reduce-scatter.3
where the time goes:
time: 513 us; the launch traced here: 512 us
  blocking collectives  221 us (43%)
  waiting for transfers between devices  151 us (29%)
  local copies, waits for them, and re-layouts  97.7 us (19%)
  between operations  14.2 us (3%)
  matrix products  11.8 us (2%)
  other arithmetic  9.8 us (2%)
  loops' own time  6.02 us (1%)
    unnamed x2, waiting for transfers between devices  151 us
    psum x1, blocking collectives, on_device(): shell_total = lax.psum(term_one + term_two + term_three, ('dom', 'orient'))  102 us
    unnamed x28, local copies, waits for them, and re-layouts  81.4 us
    psum x1, blocking collectives, on_device(): ctf_weights = lax.psum(ctf_part, 'dom')  63.1 us
    pmax x1, blocking collectives, on_device(): peak = lax.pmax(local_peak, 'orient')  30.6 us
    psum x1, blocking collectives, on_device(): lax.psum(jnp.sum(jnp.exp(scores - peak[:, None, None]), axis=(1, 2)), 'or...  25.8 us
  transfers between devices with their start and end apart: 1, of which 1 were waited for; matrix products, arithmetic and copies ran while one was open for 1% of the time, Pallas kernels for 0%

commit v1 on v0

--- a/solution.py
+++ b/solution.py
@@ -93,7 +93,9 @@
         jnp.sum(image_sums * ref_cols, axis=(0, 1)), pick_cols, precision=highest
     )
     ctf_weights = lax.psum(ctf_part, "dom")
-    shell_total = lax.psum(term_one + term_two + term_three, ("dom", "orient"))
+    shell_total = jnp.sum(
+        lax.all_gather(term_one + term_two + term_three, ("dom", "orient")), axis=0
+    )
     divisor = part_dev * dom_size * pixels / shells
     return (posterior, image_sums, ctf_weights, shell_total / divisor)
 

time: 513 us -> 680 us (1.33)
  waiting for transfers between devices: 151 us -> 420 us
  blocking collectives: 221 us -> 116 us
    unnamed x2 -> x4, waiting for transfers between devices: 151 us -> 420 us
    psum x1 -> x0, blocking collectives: 102 us -> none  [on_device(): shell_total = lax.psum(term_one + term_two + term_three, ('dom', 'orient'))]
    unnamed x28 -> x32, local copies, waits for them, and re-layouts: 81.4 us -> 82.2 us
  transfers between devices with their start and end apart: 1 -> 2, of which waited for: 1 -> 2; matrix products, arithmetic and copies ran while one was open for 1% -> 1% of each run, Pallas kernels for 0% -> 0%
where the time goes in v1:
time: 680 us; the launch traced here: 678 us
  waiting for transfers between devices  420 us (62%)
  blocking collectives  116 us (17%)
  local copies, waits for them, and re-layouts  99.6 us (15%)
  between operations  14.3 us (2%)
  matrix products  11.8 us (2%)
  other arithmetic  9.89 us (1%)
    unnamed x4, waiting for transfers between devices  420 us
    unnamed x32, local copies, waits for them, and re-layouts  82.2 us
    psum x1, blocking collectives, on_device(): ctf_weights = lax.psum(ctf_part, 'dom')  60 us
    pmax x1, blocking collectives, on_device(): peak = lax.pmax(local_peak, 'orient')  30.6 us
    psum x1, blocking collectives, on_device(): lax.psum(jnp.sum(jnp.exp(scores - peak[:, None, None]), axis=(1, 2)), 'or...  25.8 us
  transfers between devices with their start and end apart: 2, of which 2 were waited for; matrix products, arithmetic and copies ran while one was open for 1% of the time, Pallas kernels for 0%

profile of v1, /device:TPU:1, one launch (start us, length us, event | category | flops | bytes accessed | tf_op | source)
XLA Modules:
  0.0 678.0 jit_solution(8481381124698453216)
XLA Ops:
  7.3 0.7 broadcast_compare_fusion
  8.0 1.1 copy_convert_fusion
  9.1 2.8 fusion.46
  12.0 0.7 fusion.15
  12.7 1.9 multiply_reduce_fusion
  14.6 1.1 copy.28
  15.7 1.1 fusion.14
  17.1 0.7 fusion.16
  18.0 21.1 %while.24 = (s32[]{:T(128)}, f32[8,8,2,16]{3,1,2,0:T(8,128)S(1)}, f32[8,8192]{1,0:T(8,128)S(1)}, f32[8,2,8192]{2,0,1:T(8,128)S(1)}, s32[8]{0:T(128)S(1)}, /*inde...) while((s32[]{:T(128)}, f32[8,8,2,16]{3,1,2,0:T(8,128)S(1)}, ...), condition=%wide.region_2.3_spmd, body=%wide.region_1.2_spmd.sunk | while | flops 9961734 | bytes 5910755 | solution.py:60
  19.5 0.8 copy-done.4
  22.2 0.8 copy-done.4
  24.8 0.8 copy-done.4
  27.4 0.8 copy-done.4
  30.1 0.8 copy-done.4
  32.7 0.8 copy-done.4
  35.3 0.8 copy-done.4
  38.0 0.8 copy-done.4
  39.2 30.6 %pmax.7 = f32[8]{0:T(128)S(1)} all-reduce(f32[8]{0:T(128)S(1)} %select_reduce_fusion), channel_id=1, replica_groups=mesh['dom'=32,'orient'=16] {'orient'}, use_global_device_ids=true, to_apply=%region_4.5 | all-reduce | flops 8 | bytes 64 | tf_op jit(solution)/shard_map/pmax | solution.py:64
  70.0 25.8 %psum.14 = f32[8]{0:T(128)S(1)} all-reduce(f32[8]{0:T(128)S(1)} %fusion.30), channel_id=1, replica_groups=mesh['dom'=32,'orient'=16] {'orient'}, use_global_device_ids=true, to_apply=%region_6.7 | all-reduce | flops 8 | bytes 64 | tf_op jit(solution)/shard_map/psum | solution.py:65
  96.6 6.0 while.25
  102.6 31.4 %copy.34 = f32[16,2,8192]{1,0,2:T(8,128)} copy(f32[16,2,8192]{2,0,1:T(8,128)S(1)} %get-tuple-element.176) | data formatting | bytes 2097152
  134.0 46.1 %reshape.88 = f32[8192,32]{1,0:T(8,128)} reshape(f32[8192,16,2]{2,1,0:T(8,128)} %bitcast.18) | data formatting | bytes 2097152
  181.2 1.1 fusion.18
  182.8 0.9 multiply_reduce_fusion.3
  183.7 1.1 iota_compare_fusion
  184.7 213.3 %reduce-scatter.4.cloned.1.call-done = f32[256,32]{1,0:T(8,128)} async-done(((f32[8192,32]{1,0:T(8,128)}), f32[256,32]{1,0:T(8,128)}) %reduce-scatter.4.cloned.1.call-update) | async-done | bytes 32784
  398.1 2.1 reshape.89
  400.2 1.0 copy.35
  401.3 0.8 fusion.21
  403.2 60.0 %psum.15 = f32[16,64]{1,0:T(8,128)} all-reduce(f32[16,64]{1,0:T(8,128)S(1)} %get-tuple-element.318), channel_id=1, replica_groups=mesh['dom'=32,'orient'=16] {'dom'}, use_global_device_ids=true, to_apply=%region_11.12 | all-reduce | flops 1024 | bytes 8192 | tf_op jit(solution)/shard_map/psum | solution.py:95
  463.2 206.4 %all-reduce.3.cloned.1.call-done = f32[32768]{0:T(1024)} async-done(((f32[32768]{0:T(1024)}), f32[32768]{0:T(1024)}) %all-reduce.3.cloned.1.call-update) | async-done | bytes 131088
  669.6 1.0 reshape.77
  (135 shorter events, 19.7 us)
Async XLA Ops:
  7.2 9.6 %copy-start = (f32[64,64]{1,0:T(8,128)S(1)}, f32[64,64]{1,0:T(8,128)}, u32[]{:S(2)}) copy-start(f32[64,64]{1,0:T(8,128)} %param.17) | copy-start | bytes 49156
  7.2 4.7 copy-start.8
  7.2 4.7 copy-start.13
  7.2 5.5 copy-start.1
  7.2 390.9 %reduce-scatter.4.cloned.1.call-start = ((), (), s32[]{:S(2)}) async-start(), calls=%async_computation.2 | async-start | bytes 4325376
  11.9 4.9 copy-start.12
  17.1 0.9 copy-start.6
  19.2 1.0 copy-start.4
  21.9 1.0 copy-start.4
  24.5 1.0 copy-start.4
  27.2 1.0 copy-start.4
  29.8 1.0 copy-start.4
  32.4 1.0 copy-start.4
  35.0 1.0 copy-start.4
  37.7 1.0 copy-start.4
  95.8 0.8 copy-start.10
  180.1 0.7 copy-start.11
  180.1 1.0 copy-start.3
  180.1 1.1 copy-start.9
  180.1 2.2 copy-start.2
  180.2 489.4 %all-reduce.3.cloned.1.call-start = ((), (), s32[]{:S(2)}) async-start(), calls=%async_computation.1 | async-start | bytes 262144
  401.3 269.9 %copy-start.7 = (f32[16,2,256]{2,1,0:T(2,128)}, f32[16,2,256]{2,1,0:T(2,128)S(1)}, u32[]{:S(2)}) copy-start(f32[16,2,256]{2,1,0:T(2,128)S(1)} %copy.35) | copy-start | bytes 98308
  402.5 0.7 copy-start.5
Sparse Core Ops, SparseCore 0:
  180.3 217.7 reduce-scatter.3
  403.8 265.7 all-reduce.2
